TPU v7x, 128 devices: a whole 4x4x4 slice. The times are simulated.
128 devices in a mesh: head: 4 (over y_hi, core), seq: 32 (over z, y_lo, x).
Axes of the slice: x: 4, y: 4 (y_hi: 2, y_lo: 2; y = y_hi * 2 + y_lo), z: 4, core: 2. Of those that a mesh axis runs over, the one named last changes fastest.
Arguments:
- cached_keys: bfloat16 [32, 32768, 8, 128], P(None, 'seq', 'head'), may hold values from -6 to 6
- queries: bfloat16 [32, 64, 128], P('seq', 'head'), may hold values from -6 to 6
- seq_lengths: int32 [32], replicated, may hold values from 1 to 32768
Outputs:
- page_min: bfloat16 [32, 2048, 8, 128], P('seq', 'head')
- page_max: bfloat16 [32, 2048, 8, 128], P('seq', 'head')
- page_mean: float32 [32, 2048, 8, 128], P('seq', 'head')
- page_score: float32 [32, 64, 2048], P('seq', None, 'head')
All inputs are finite; a program needn't handle non-finite values.
Results may differ from a plain program's by a relative error of at most 0.001.
Values may be sent and summed in bfloat16 or wider, within the bound.
No kernel may reach another device: no remote copies, remote signals or barrier semaphores. Data moves between devices by JAX's collectives and lax.ppermute only.
A program may use at most 192 MiB of HBM per device.

v0:
```python
import jax
import jax.numpy as jnp
from jax import lax
from jax.sharding import PartitionSpec as P

PAGE = 16


def copy_for_each(x, axis):
    length = lax.axis_size(axis)
    return lax.all_to_all(jnp.broadcast_to(x[None], (length, *x.shape)), axis, 0, 0, tiled=True)


def in_order(parts, dim):
    shape = list(parts.shape[1:])
    shape[dim] *= parts.shape[0]
    return jnp.moveaxis(parts, 0, dim).reshape(shape)


def collect(x, axis, dim):
    parts = copy_for_each(x, axis)
    return in_order(parts, dim)


def page_bounds(block, start, limit):
    seq_count = block.shape[0]
    tokens = block.shape[1]
    position = start + jnp.arange(tokens, dtype=jnp.int32)
    live_token = (position[None, :] < limit[:, None])[:, :, None, None]
    shaped = (seq_count, tokens // PAGE, PAGE, block.shape[2], block.shape[3])
    top_value = jnp.array(jnp.inf, block.dtype)
    lower = jnp.min(jnp.where(live_token, block, top_value).reshape(shaped), axis=2)
    upper = jnp.max(jnp.where(live_token, block, -top_value).reshape(shaped), axis=2)
    key_sums = jnp.sum(
        jnp.where(live_token, block, jnp.zeros((), block.dtype)).reshape(shaped),
        axis=2,
        dtype=jnp.float32,
    )
    page_start = start + PAGE * jnp.arange(tokens // PAGE, dtype=jnp.int32)
    page_live = (page_start[None, :] < limit[:, None])[:, :, None, None]
    zero_value = jnp.zeros((), block.dtype)
    lower = jnp.where(page_live, lower, zero_value)
    upper = jnp.where(page_live, upper, zero_value)
    return (lower, upper, key_sums)


def page_average(key_sums, start, limit):
    page_start = start + PAGE * jnp.arange(key_sums.shape[1], dtype=jnp.int32)
    counts = jnp.clip(limit[:, None] - page_start[None, :], 0, PAGE).astype(jnp.float32)
    return key_sums / jnp.maximum(counts, 1.0)[:, :, None, None]


def bound_scores(query, lower, upper):
    seq_count, heads, width = query.shape
    kv_heads = lower.shape[2]
    grouped = query.astype(jnp.float32).reshape(seq_count, kv_heads, heads // kv_heads, width)
    positive = jnp.maximum(grouped, 0.0)
    negative = jnp.minimum(grouped, 0.0)
    score = jnp.einsum(
        "shgc,sphc->shgp", positive, upper.astype(jnp.float32), precision=lax.Precision.HIGHEST
    )
    score = score + jnp.einsum(
        "shgc,sphc->shgp", negative, lower.astype(jnp.float32), precision=lax.Precision.HIGHEST
    )
    return score.reshape(seq_count, heads, lower.shape[1]) * width ** (-0.5)


def local(cached_keys, queries, seq_lengths):
    seq_index = lax.axis_index("seq")
    head_index = lax.axis_index("head")
    local_seqs = cached_keys.shape[0] // lax.axis_size("seq")
    block_tokens = cached_keys.shape[1]
    quarter = block_tokens * lax.axis_size("seq") // lax.axis_size("head")
    first_token = head_index * quarter
    my_lengths = lax.dynamic_slice_in_dim(seq_lengths, seq_index * local_seqs, local_seqs)
    block_start = seq_index * block_tokens
    lower, upper, key_sums = page_bounds(cached_keys, block_start, seq_lengths)
    lower, upper = (
        lax.all_to_all(
            lax.all_to_all(lower, "seq", split_axis=0, concat_axis=1, tiled=True),
            "head",
            split_axis=1,
            concat_axis=2,
            tiled=True,
        ),
        lax.all_to_all(
            lax.all_to_all(upper, "seq", split_axis=0, concat_axis=1, tiled=True),
            "head",
            split_axis=1,
            concat_axis=2,
            tiled=True,
        ),
    )
    key_sums = lax.all_to_all(
        lax.all_to_all(key_sums, "seq", split_axis=0, concat_axis=1, tiled=True),
        "head",
        split_axis=1,
        concat_axis=2,
        tiled=True,
    )
    average = page_average(key_sums, first_token, my_lengths)
    whole_query = collect(queries, "head", 1)
    score = bound_scores(whole_query, lower, upper)
    return (lower, upper, average, score)


def solution(mesh):
    return jax.shard_map(
        local,
        mesh=mesh,
        in_specs=(P(None, "seq", "head", None), P("seq", "head", None), P()),
        out_specs=(
            P("seq", "head", None, None),
            P("seq", "head", None, None),
            P("seq", "head", None, None),
            P("seq", None, "head"),
        ),
        check_vma=False,
    )
```

profile of v0, /device:TPU:1, one launch (start us, length us, event | category | flops | bytes accessed | tf_op | source)
XLA Modules:
  0.0 260.6 jit_solution(9636246986457096856)
XLA Ops:
  0.6 1.3 broadcast_in_dim.64
  1.9 6.0 %all-to-all-start.6 = ((bf16[4,1,16,128]{3,2,1,0:T(8,128)(2,1)}), bf16[4,1,16,128]{3,2,1,0:T(8,128)(2,1)S(1)}, u32[]{:S(2)}, u32[]{:S(2)}) async-start(bf16[4,1,16,128]{3,2,1,0:T(8,128)(2,1)} %broadcast_in_dim.64), calls=%async_computation.6 | async-start | bytes 32768 | tf_op jit(solution)/shard_map/all_to_all | solution.py:11
  7.9 0.7 broadcast_compare_fusion
  9.4 53.1 %broadcast_select_fusion = (bf16[32,1024,2,128]{3,2,1,0:T(2,128)(2,1)}, bf16[32,1024,2,128]{3,2,1,0:T(2,128)(2,1)}, bf16[32,1024,2,128]{3,2,1,0:T(2,128)(2,1)}) fusion(bf16[32,1024,2,128]{3,2,1,0:T(2,128)(2,1)} %param.3, pred[32,1024]{1,0:T(8,128)(4,1)S(1)} %broadcast_compare_fusion), kind=kLoop, calls=%fused_computation.1 | loop fusion | flops 25165824 | bytes 67141632 | tf_op jit(solution)/shard_map/jit(_where)/select_n | solution.py:35
  62.5 18.5 %reduce_max.9 = bf16[32,64,2,128]{3,2,1,0:T(2,128)(2,1)S(1)} reduce(bf16[32,64,16,2,128]{4,3,2,1,0:T(2,128)(2,1)} %bitcast.32, bf16[]{:T(256)} %constant.5.clone.1), dimensions={2}, to_apply=%region_1.2 | reduce | flops 7864320 | bytes 17825794 | tf_op jit(solution)/shard_map/reduce_max | solution.py:33
  81.0 18.5 %reduce_min.9 = bf16[32,64,2,128]{3,2,1,0:T(2,128)(2,1)S(1)} reduce(bf16[32,64,16,2,128]{4,3,2,1,0:T(2,128)(2,1)} %bitcast.31, bf16[]{:T(256)} %constant.3.clone.1), dimensions={2}, to_apply=%region_0.1 | reduce | flops 7864320 | bytes 17825794 | tf_op jit(solution)/shard_map/reduce_min | solution.py:32
  99.6 2.9 %broadcast_select_fusion.3 = (bf16[32,64,2,128]{3,2,1,0:T(2,128)(2,1)S(1)}, bf16[32,64,2,128]{3,2,1,0:T(2,128)(2,1)S(1)}) fusion(bf16[32,64,2,128]{3,2,1,0:T(2,128)(2,1)S(1)} %reduce_max.9, pred[32,64]{1,0:T(8,128)(4,1)S(1)} %broadcast_compare_fusion.1, bf16[32,64,2,128]{3,2,1,0:T(2,128)(2,1)S(1)} %reduce_min.9), kind=kLoop, calls=%fused_computation.4 | loop fusion | flops 1048576 | bytes 4196352 | tf_op jit(solution)/shard_map/jit(_where)/select_n | solution.py:43
  102.5 1.2 copy.38
  103.7 8.0 %all-to-all-start.2 = ((bf16[32,64,2,128]{3,1,2,0:T(8,128)(2,1)}), bf16[32,64,2,128]{3,1,2,0:T(8,128)(2,1)S(1)}, u32[]{:S(2)}, u32[]{:S(2)}) async-start(bf16[32,64,2,128]{3,1,2,0:T(8,128)(2,1)} %copy.38), calls=%async_computation.2 | async-start | bytes 2097152 | tf_op jit(solution)/shard_map/all_to_all | solution.py:87
  111.7 1.2 copy.33
  113.0 14.9 %all-to-all-done.2 = bf16[32,64,2,128]{3,1,2,0:T(8,128)(2,1)S(1)} async-done(((bf16[32,64,2,128]{3,1,2,0:T(8,128)(2,1)}), bf16[32,64,2,128]{3,1,2,0:T(8,128)(2,1)S(1)}, u32[]{:S(2)}, u32[]{:S(2)}) %all-to-all-start.2) | async-done | bytes 1048608 | tf_op jit(solution)/shard_map/all_to_all | solution.py:87
  127.9 4.9 %all-to-all-start = ((bf16[32,64,2,128]{3,1,2,0:T(8,128)(2,1)}), bf16[32,64,2,128]{3,1,2,0:T(8,128)(2,1)S(1)}, u32[]{:S(2)}, u32[]{:S(2)}) async-start(bf16[32,64,2,128]{3,1,2,0:T(8,128)(2,1)} %copy.33), calls=%async_computation | async-start | bytes 2097152 | tf_op jit(solution)/shard_map/all_to_all | solution.py:80
  132.9 9.5 %copy.40 = bf16[1,2048,2,128]{3,2,0,1:T(2,128)(2,1)} copy(bf16[1,2048,2,128]{3,1,2,0:T(8,128)(2,1)S(1)} %bitcast.41) | data formatting | bytes 2097152 | tf_op jit(solution)/shard_map/all_to_all | solution.py:87
  142.4 5.0 %all-to-all-done = bf16[32,64,2,128]{3,1,2,0:T(8,128)(2,1)S(1)} async-done(((bf16[32,64,2,128]{3,1,2,0:T(8,128)(2,1)}), bf16[32,64,2,128]{3,1,2,0:T(8,128)(2,1)S(1)}, u32[]{:S(2)}, u32[]{:S(2)}) %all-to-all-start) | async-done | bytes 1048608 | tf_op jit(solution)/shard_map/all_to_all | solution.py:80
  147.4 8.1 %all-to-all-start.3 = ((bf16[1,2048,2,128]{3,2,0,1:T(2,128)(2,1)}), bf16[1,2048,2,128]{3,2,0,1:T(2,128)(2,1)S(1)}, u32[]{:S(2)}, u32[]{:S(2)}) async-start(bf16[1,2048,2,128]{3,2,0,1:T(2,128)(2,1)} %copy.40), calls=%async_computation.3 | async-start | bytes 2097152 | tf_op jit(solution)/shard_map/all_to_all | solution.py:86
  155.5 16.7 %convert_reduce_fusion = f32[32,64,2,128]{3,2,1,0:T(2,128)S(1)} fusion(bf16[32,64,16,2,128]{4,3,2,1,0:T(2,128)(2,1)} %bitcast.33), kind=kLoop, calls=%fused_computation | loop fusion | flops 16252928 | bytes 18874368 | tf_op jit(solution)/shard_map/reduce_sum | solution.py:34
  172.2 1.6 copy.43
  173.8 4.3 %all-to-all-start.4 = ((f32[32,64,2,128]{3,1,2,0:T(8,128)}), f32[32,64,2,128]{3,1,2,0:T(8,128)S(1)}, u32[]{:S(2)}, u32[]{:S(2)}) async-start(f32[32,64,2,128]{3,1,2,0:T(8,128)} %copy.43), calls=%async_computation.4 | async-start | bytes 4194304 | tf_op jit(solution)/shard_map/all_to_all | solution.py:95
  178.1 1.3 copy.34
  179.4 9.5 %copy.35 = bf16[1,2048,2,128]{3,2,0,1:T(2,128)(2,1)} copy(bf16[1,2048,2,128]{3,1,2,0:T(8,128)(2,1)S(1)} %bitcast.42) | data formatting | bytes 2097152 | tf_op jit(solution)/shard_map/all_to_all | solution.py:80
  188.9 16.6 %all-to-all-done.4 = f32[32,64,2,128]{3,1,2,0:T(8,128)S(1)} async-done(((f32[32,64,2,128]{3,1,2,0:T(8,128)}), f32[32,64,2,128]{3,1,2,0:T(8,128)S(1)}, u32[]{:S(2)}, u32[]{:S(2)}) %all-to-all-start.4) | async-done | bytes 2097184 | tf_op jit(solution)/shard_map/all_to_all | solution.py:95
  205.5 6.2 %all-to-all-start.1 = ((bf16[1,2048,2,128]{3,2,0,1:T(2,128)(2,1)}), bf16[1,2048,2,128]{3,2,0,1:T(2,128)(2,1)}, u32[]{:S(2)}, u32[]{:S(2)}) async-start(bf16[1,2048,2,128]{3,2,0,1:T(2,128)(2,1)} %copy.35), calls=%async_computation.1 | async-start | bytes 2097152 | tf_op jit(solution)/shard_map/all_to_all | solution.py:79
  212.0 8.6 %copy.45 = f32[1,2048,2,128]{3,2,0,1:T(2,128)} copy(f32[1,2048,2,128]{3,1,2,0:T(8,128)S(1)} %bitcast.39) | data formatting | bytes 4194304 | tf_op jit(solution)/shard_map/all_to_all | solution.py:95
  220.5 6.3 %all-to-all-done.1 = bf16[1,2048,2,128]{3,2,0,1:T(2,128)(2,1)} async-done(((bf16[1,2048,2,128]{3,2,0,1:T(2,128)(2,1)}), bf16[1,2048,2,128]{3,2,0,1:T(2,128)(2,1)}, u32[]{:S(2)}, u32[]{:S(2)}) %all-to-all-start.1) | async-done | bytes 1048608 | tf_op jit(solution)/shard_map/all_to_all | solution.py:79
  226.8 4.5 %all-to-all-start.5 = ((f32[1,2048,2,128]{3,2,0,1:T(2,128)}), f32[1,2048,2,128]{3,2,0,1:T(2,128)S(1)}, u32[]{:S(2)}, u32[]{:S(2)}) async-start(f32[1,2048,2,128]{3,2,0,1:T(2,128)} %copy.45), calls=%async_computation.5 | async-start | bytes 4194304 | tf_op jit(solution)/shard_map/all_to_all | solution.py:94
  232.8 1.4 copy.36
  234.3 1.6 copy.50
  235.9 1.6 copy.51
  237.6 0.9 fusion.2
  238.5 1.6 fusion.1
  240.1 17.5 %all-to-all-done.5 = f32[1,2048,2,128]{3,2,0,1:T(2,128)S(1)} async-done(((f32[1,2048,2,128]{3,2,0,1:T(2,128)}), f32[1,2048,2,128]{3,2,0,1:T(2,128)S(1)}, u32[]{:S(2)}, u32[]{:S(2)}) %all-to-all-start.5) | async-done | bytes 2097184 | tf_op jit(solution)/shard_map/all_to_all | solution.py:94
  258.1 2.5 copy.52
  (20 shorter events, 3.1 us)
Async XLA Ops:
  1.9 101.8 %all-to-all-start.6 = ((bf16[4,1,16,128]{3,2,1,0:T(8,128)(2,1)}), bf16[4,1,16,128]{3,2,1,0:T(8,128)(2,1)S(1)}, u32[]{:S(2)}, u32[]{:S(2)}) async-start(bf16[4,1,16,128]{3,2,1,0:T(8,128)(2,1)} %broadcast_in_dim.64), calls=%async_computation.6 | async-start | bytes 32768 | tf_op jit(solution)/shard_map/all_to_all | solution.py:11
  103.7 24.1 %all-to-all-start.2 = ((bf16[32,64,2,128]{3,1,2,0:T(8,128)(2,1)}), bf16[32,64,2,128]{3,1,2,0:T(8,128)(2,1)S(1)}, u32[]{:S(2)}, u32[]{:S(2)}) async-start(bf16[32,64,2,128]{3,1,2,0:T(8,128)(2,1)} %copy.38), calls=%async_computation.2 | async-start | bytes 2097152 | tf_op jit(solution)/shard_map/all_to_all | solution.py:87
  127.9 19.5 %all-to-all-start = ((bf16[32,64,2,128]{3,1,2,0:T(8,128)(2,1)}), bf16[32,64,2,128]{3,1,2,0:T(8,128)(2,1)S(1)}, u32[]{:S(2)}, u32[]{:S(2)}) async-start(bf16[32,64,2,128]{3,1,2,0:T(8,128)(2,1)} %copy.33), calls=%async_computation | async-start | bytes 2097152 | tf_op jit(solution)/shard_map/all_to_all | solution.py:80
  147.4 8.1 %copy-start = (bf16[32,64,2,128]{3,1,2,0:T(8,128)(2,1)}, bf16[32,64,2,128]{3,1,2,0:T(8,128)(2,1)S(1)}, u32[]{:S(2)}) copy-start(bf16[32,64,2,128]{3,1,2,0:T(8,128)(2,1)S(1)} %all-to-all-done) | copy-start | bytes 3145732
  147.4 26.5 %all-to-all-start.3 = ((bf16[1,2048,2,128]{3,2,0,1:T(2,128)(2,1)}), bf16[1,2048,2,128]{3,2,0,1:T(2,128)(2,1)S(1)}, u32[]{:S(2)}, u32[]{:S(2)}) async-start(bf16[1,2048,2,128]{3,2,0,1:T(2,128)(2,1)} %copy.40), calls=%async_computation.3 | async-start | bytes 2097152 | tf_op jit(solution)/shard_map/all_to_all | solution.py:86
  172.2 59.1 %copy-start.1 = (s32[32]{0:T(128)S(1)}, s32[32]{0:T(128)}, u32[]{:S(2)}) copy-start(s32[32]{0:T(128)} %param.5) | copy-start | bytes 388
  173.8 31.7 %all-to-all-start.4 = ((f32[32,64,2,128]{3,1,2,0:T(8,128)}), f32[32,64,2,128]{3,1,2,0:T(8,128)S(1)}, u32[]{:S(2)}, u32[]{:S(2)}) async-start(f32[32,64,2,128]{3,1,2,0:T(8,128)} %copy.43), calls=%async_computation.4 | async-start | bytes 4194304 | tf_op jit(solution)/shard_map/all_to_all | solution.py:95
  205.5 21.3 %all-to-all-start.1 = ((bf16[1,2048,2,128]{3,2,0,1:T(2,128)(2,1)}), bf16[1,2048,2,128]{3,2,0,1:T(2,128)(2,1)}, u32[]{:S(2)}, u32[]{:S(2)}) async-start(bf16[1,2048,2,128]{3,2,0,1:T(2,128)(2,1)} %copy.35), calls=%async_computation.1 | async-start | bytes 2097152 | tf_op jit(solution)/shard_map/all_to_all | solution.py:79
  226.8 30.8 %all-to-all-start.5 = ((f32[1,2048,2,128]{3,2,0,1:T(2,128)}), f32[1,2048,2,128]{3,2,0,1:T(2,128)S(1)}, u32[]{:S(2)}, u32[]{:S(2)}) async-start(f32[1,2048,2,128]{3,2,0,1:T(2,128)} %copy.45), calls=%async_computation.5 | async-start | bytes 4194304 | tf_op jit(solution)/shard_map/all_to_all | solution.py:94
where the time goes:
time: 262 us; the launch traced here: 261 us
  other arithmetic  112 us (43%)
  waiting for transfers between devices  60.3 us (23%)
  local copies, waits for them, and re-layouts  42.8 us (16%)
  starting transfers between devices  42 us (16%)
    select_n x1, other arithmetic, page_bounds(): jnp.where(live_token, block, jnp.zeros((), block.dtype)).reshape(shaped)  53.1 us
    reduce_max x1, other arithmetic, page_bounds(): jnp.max(jnp.where(live_token, block, -top_value).reshape(shaped), axis=2)  18.5 us
    reduce_min x1, other arithmetic, page_bounds(): jnp.min(jnp.where(live_token, block, top_value).reshape(shaped), axis=2)  18.5 us
    all_to_all x1, waiting for transfers between devices, local(): lax.all_to_all(lax.all_to_all(key_sums, 'seq', split_axis=0, concat_axis=...  17.5 us
    reduce_sum x1, other arithmetic, page_bounds(): jnp.sum(jnp.where(live_token, block, jnp.zeros((), block.dtype)).reshape(...  16.7 us
    all_to_all x1, waiting for transfers between devices, local(): lax.all_to_all(key_sums, 'seq', split_axis=0, concat_axis=1, tiled=True)  16.6 us
    all_to_all x1, waiting for transfers between devices, local(): lax.all_to_all(upper, 'seq', split_axis=0, concat_axis=1, tiled=True)  14.9 us
    all_to_all x2, local copies, waits for them, and re-layouts, local(): lax.all_to_all(lower, 'seq', split_axis=0, concat_axis=1, tiled=True)  10.8 us
  transfers between devices with their start and end apart: 7, of which 5 were waited for; matrix products, arithmetic and copies ran while one was open for 59% of the time, Pallas kernels for 0%

commit v1 on v0

v1 whole, which is shorter than its diff:
```python
import functools

import jax
import jax.numpy as jnp
from jax import lax
from jax.experimental import pallas as pl
from jax.experimental.pallas import tpu as pltpu
from jax.sharding import PartitionSpec as P

PAGE = 16
F32 = jnp.float32
BF16 = jnp.bfloat16
GROUP = 8
STEP = 2.0**-10


def merge(u, w, mask, shift, op):
    low = jnp.where(mask, u, w)
    high = jnp.where(mask, w, u)
    return op(low, pltpu.roll(high, shift, 0))


def fold_pages(pages, masks, op):
    a, b, c, d = masks["8"], masks["8s4"], masks["8s2"], masks["8s6"]
    left = merge(
        merge(pages[3], pages[7], a, 8, op), merge(pages[1], pages[5], b, 8, op), masks["4"], 4, op
    )
    right = merge(
        merge(pages[2], pages[6], c, 8, op), merge(pages[0], pages[4], d, 8, op), masks["4s2"], 4, op
    )
    return merge(left, right, masks["2"], 2, op)


def fold_masks():
    row = lax.broadcasted_iota(jnp.int32, (16, 128), 0)
    return {
        "8": row < 8,
        "8s4": (row + 4) % 16 < 8,
        "8s2": (row + 2) % 16 < 8,
        "8s6": (row + 6) % 16 < 8,
        "4": row % 8 >= 4,
        "4s2": (row + 2) % 8 >= 4,
        "2": row % 4 >= 2,
    }


def encode(sums, lower, upper):
    reach = 16.0 * jnp.maximum(upper, -lower)
    ratio = sums / jnp.maximum(reach, 2.0**-120)
    size = jnp.abs(ratio)
    head = size.astype(BF16).astype(F32)
    rest = size - head
    unit = head * STEP
    left = jnp.abs(rest)
    two = left > 2.0 * unit
    left = jnp.where(two, left - 2.0 * unit, left)
    band = jnp.where(rest > 0.0, 2.0**30, 2.0**-90)
    band = jnp.where(two, band * 2.0**60, band)
    band = jnp.where(left > unit, band * 2.0**30, band)
    code = head * band
    code = jnp.where(size < 2.0**-29, 0.0, code)
    return jnp.where(ratio < 0.0, -code, code)


def decode(code, lower, upper):
    size = jnp.abs(code)
    four = size >= 2.0
    size = jnp.where(four, size * 2.0**-120, size)
    two = size >= 2.0**-59
    size = jnp.where(two, size * 2.0**-60, size)
    one = size >= 2.0**-89
    size = jnp.where(one, size * 2.0**-30, size)
    more = jnp.where(two, 2.5 * STEP, 0.5 * STEP) + jnp.where(one, STEP, 0.0)
    head = size * 2.0**90
    size = head + head * jnp.where(four, more, -more)
    value = jnp.where(code < 0.0, -size, size)
    return value * (16.0 * jnp.maximum(upper, -lower))


def reduce_kernel(tokens, lengths_ref, x_ref, pick_ref, out_ref):
    limit = lengths_ref[pl.program_id(0)] - lax.axis_index("seq") * tokens
    rows = 2 * PAGE * GROUP

    def run(masked):
        masks = fold_masks()
        pick = pick_ref[...]
        for g in range(tokens // PAGE // GROUP):
            x = x_ref[g * rows : (g + 1) * rows, :]
            low = high = x
            if masked:
                row = lax.broadcasted_iota(jnp.int32, (rows, 128), 0) + g * rows
                live = row < 2 * limit
                low = jnp.where(live, x, jnp.array(jnp.inf, BF16))
                high = jnp.where(live, x, jnp.array(-jnp.inf, BF16))
                x = jnp.where(live, x, jnp.zeros((), BF16))
            sums = jnp.dot(pick, x, preferred_element_type=F32)
            lows, highs = [], []
            for j in range(GROUP):
                first = slice(32 * j, 32 * j + 16)
                second = slice(32 * j + 16, 32 * j + 32)
                lows.append(jnp.minimum(low[first], low[second]))
                highs.append(jnp.maximum(high[first], high[second]))
            lower = fold_pages(lows, masks, jnp.minimum).astype(F32)
            upper = fold_pages(highs, masks, jnp.maximum).astype(F32)
            if masked:
                row = lax.broadcasted_iota(jnp.int32, (16, 128), 0)
                page = row // 2 + g * GROUP
                live = page * PAGE < limit
                lower = jnp.where(live, lower, 0.0)
                upper = jnp.where(live, upper, 0.0)
            at = slice(16 * g, 16 * g + 16)
            out_ref[0, 0, at, :] = lower.astype(BF16)
            out_ref[0, 1, at, :] = upper.astype(BF16)
            out_ref[0, 2, at, :] = encode(sums, lower, upper).astype(BF16)

    @pl.when(limit >= tokens)
    def _():
        run(False)

    @pl.when((limit > 0) & (limit < tokens))
    def _():
        run(True)

    @pl.when(limit <= 0)
    def _():
        out_ref[...] = jnp.zeros_like(out_ref)


def reduce_pages(keys, lengths):
    seqs, tokens, heads, width = keys.shape
    pages = tokens // PAGE
    flat = keys.reshape(seqs * tokens * heads, width)
    rows = 2 * PAGE * GROUP
    r = jnp.arange(2 * GROUP, dtype=jnp.int32)[:, None]
    k = jnp.arange(rows, dtype=jnp.int32)[None, :]
    pick = ((k // (2 * PAGE) == r // 2) & (k % 2 == r % 2)).astype(BF16)
    return pl.pallas_call(
        functools.partial(reduce_kernel, tokens),
        grid_spec=pltpu.PrefetchScalarGridSpec(
            num_scalar_prefetch=1,
            grid=(seqs,),
            in_specs=[
                pl.BlockSpec((tokens * heads, width), lambda s, n: (s, 0)),
                pl.BlockSpec((2 * GROUP, rows), lambda s, n: (0, 0)),
            ],
            out_specs=pl.BlockSpec((1, 3, pages * heads, width), lambda s, n: (s, 0, 0, 0)),
        ),
        out_shape=jax.ShapeDtypeStruct((seqs, 3, pages * heads, width), BF16),
        name="reduce_pages",
    )(lengths, flat, pick)


def finish_kernel(
    pages, lengths_ref, in_ref, query_ref, low_ref, high_ref, mean_ref, score_ref, low_f, high_f, pair_f
):
    me = lax.axis_index("head")
    step = pl.program_id(0)
    sources, parts, _, rows, width = in_ref.shape
    total = parts * rows
    here = total // 2
    first = me * pages + step * here
    limit = lengths_ref[lax.axis_index("seq")]
    page = first + lax.broadcasted_iota(jnp.int32, (total, width), 0) // 2
    count = jnp.maximum(jnp.clip(limit - page * PAGE, 0, PAGE), 1).astype(F32)
    nt = (((1,), (1,)), ((), ()))
    for source in range(sources):
        query = query_ref[lax.rem(me - source + sources, sources)].astype(F32)
        lower = in_ref[source, :, 0].reshape(total, width).astype(F32)
        upper = in_ref[source, :, 1].reshape(total, width).astype(F32)
        code = in_ref[source, :, 2].reshape(total, width).astype(F32)
        pair_f[0] = lower
        pair_f[1] = upper
        pair_f[2] = decode(code, lower, upper) / count
        for h in range(2):
            kv = 2 * source + h
            every = pl.ds(h, here, stride=2)
            where = pl.ds(kv, here, stride=2 * sources)
            lo = pair_f[0, every, :]
            hi = pair_f[1, every, :]
            low_f[where, :] = lo
            high_f[where, :] = hi
            mean_ref[where, :] = pair_f[2, every, :]
            q = query[8 * h : 8 * h + 8]
            score = lax.dot_general(
                jnp.maximum(q, 0.0).astype(BF16), hi.astype(BF16), nt, preferred_element_type=F32
            )
            score += lax.dot_general(
                jnp.minimum(q, 0.0).astype(BF16), lo.astype(BF16), nt, preferred_element_type=F32
            )
            score_ref[8 * kv : 8 * kv + 8, :] = score * width ** (-0.5)
    low_ref[...] = low_f[...].astype(BF16)
    high_ref[...] = high_f[...].astype(BF16)


def finish(parts, queries, lengths):
    sources, blocks, _, rows, width = parts.shape
    heads = 2 * sources
    pages = blocks * rows // 2
    each = 2
    here = each * rows // 2
    out = lambda dtype: jax.ShapeDtypeStruct((pages * heads, width), dtype)
    flat = pl.BlockSpec((here * heads, width), lambda i, n: (i, 0))
    total_q = sources * queries.shape[1]
    return pl.pallas_call(
        functools.partial(finish_kernel, pages),
        grid_spec=pltpu.PrefetchScalarGridSpec(
            num_scalar_prefetch=1,
            grid=(blocks // each,),
            in_specs=[
                pl.BlockSpec((sources, each, 3, rows, width), lambda i, n: (0, i, 0, 0, 0)),
                pl.BlockSpec(queries.shape, lambda i, n: (0, 0, 0)),
            ],
            out_specs=[flat, flat, flat, pl.BlockSpec((total_q, here), lambda i, n: (0, i))],
            scratch_shapes=[
                pltpu.VMEM((here * heads, width), F32),
                pltpu.VMEM((here * heads, width), F32),
                pltpu.VMEM((3, each * rows, width), F32),
            ],
        ),
        out_shape=[out(BF16), out(BF16), out(F32), jax.ShapeDtypeStruct((total_q, pages), F32)],
        name="finish",
    )(lengths, parts, queries)


def local(cached_keys, queries, seq_lengths):
    head_count = lax.axis_size("head")
    seqs = cached_keys.shape[0]
    width = cached_keys.shape[3]
    packed = reduce_pages(cached_keys, seq_lengths)
    query, packed = lax.optimization_barrier((queries[0], packed))
    shifted = [query]
    for k in range(1, head_count):
        ring = [(h, (h + k) % head_count) for h in range(head_count)]
        shifted.append(lax.ppermute(query, "head", ring))
    packed = lax.all_to_all(packed, "seq", 0, 0, tiled=True)
    packed = packed.reshape(head_count, seqs // head_count, *packed.shape[1:])
    packed = lax.all_to_all(packed, "head", 0, 0, tiled=True)
    lower, upper, mean, score = finish(packed, jnp.stack(shifted), seq_lengths)
    shape = (1, -1, head_count * cached_keys.shape[2], width)
    return lower.reshape(shape), upper.reshape(shape), mean.reshape(shape), score[None]


def solution(mesh):
    return jax.shard_map(
        local,
        mesh=mesh,
        in_specs=(P(None, "seq", "head", None), P("seq", "head", None), P()),
        out_specs=(
            P("seq", "head", None, None),
            P("seq", "head", None, None),
            P("seq", "head", None, None),
            P("seq", None, "head"),
        ),
        check_vma=False,
    )
```

time: 262 us -> 126 us (0.48)
  other arithmetic: 112 us -> 1.29 us
  blocking collectives: 0 us -> 44.3 us
  local copies, waits for them, and re-layouts: 42.8 us -> 1.64 us
  Pallas kernels: 0 us -> 32.3 us
  starting transfers between devices: 42 us -> 13.2 us
  waiting for transfers between devices: 60.3 us -> 31.7 us
    all_to_all x7 -> x1, waiting for transfers between devices: 60.3 us -> 0.01 us  [local(): packed = lax.all_to_all(packed, 'head', 0, 0, tiled=True)]
    select_n x2, other arithmetic: 56 us -> 0.01 us  [reduce_pages(): pick = ((k // (2 * PAGE) == r // 2) & (k % 2 == r % 2)).astype(BF16)]
    all_to_all x0 -> x1, blocking collectives: none -> 44.3 us  [local(): packed = lax.all_to_all(packed, 'seq', 0, 0, tiled=True)]
    all_to_all x7 -> x1, starting transfers between devices: 42 us -> 6.81 us  [local(): packed = lax.all_to_all(packed, 'head', 0, 0, tiled=True)]
    pallas_call x0 -> x2, Pallas kernels: none -> 32.3 us  [the longest x1 25.3 us: reduce_pages(): pl.pallas_call(functools.partial(reduce_kernel, tokens), grid_spec=pltpu....]
    ppermute x0 -> x3, waiting for transfers between devices: none -> 31.7 us  [local(): shifted.append(lax.ppermute(query, 'head', ring))]
    all_to_all x12 -> x0, local copies, waits for them, and re-layouts: 31 us -> none  [the longest x2 10.8 us: local(): lax.all_to_all(lower, 'seq', split_axis=0, concat_axis=1, tiled=True)]
    reduce_max x1 -> x0, other arithmetic: 18.5 us -> none  [page_bounds(): jnp.max(jnp.where(live_token, block, -top_value).reshape(shaped), axis=2)]
  transfers between devices with their start and end apart: 7 -> 4, of which waited for: 5 -> 1; matrix products, arithmetic and copies ran while one was open for 59% -> 0% of each run, Pallas kernels for 0% -> 0%
where the time goes in v1:
time: 126 us; the launch traced here: 125 us
  blocking collectives  44.3 us (35%)
  Pallas kernels  32.3 us (26%)
  waiting for transfers between devices  31.7 us (25%)
  starting transfers between devices  13.2 us (10%)
  local copies, waits for them, and re-layouts  1.64 us (1%)
  other arithmetic  1.29 us (1%)
    all_to_all x1, blocking collectives, local(): packed = lax.all_to_all(packed, 'seq', 0, 0, tiled=True)  44.3 us
    ppermute x3, waiting for transfers between devices, local(): shifted.append(lax.ppermute(query, 'head', ring))  31.7 us
    pallas_call x1, Pallas kernels, reduce_pages(): pl.pallas_call(functools.partial(reduce_kernel, tokens), grid_spec=pltpu....  25.3 us
    pallas_call x1, Pallas kernels, finish(): pl.pallas_call(functools.partial(finish_kernel, pages), grid_spec=pltpu.P...  7.05 us
    all_to_all x1, starting transfers between devices, local(): packed = lax.all_to_all(packed, 'head', 0, 0, tiled=True)  6.81 us
    ppermute x3, starting transfers between devices, local(): shifted.append(lax.ppermute(query, 'head', ring))  6.39 us
  transfers between devices with their start and end apart: 4, of which 1 were waited for; matrix products, arithmetic and copies ran while one was open for 0% of the time, Pallas kernels for 0%

profile of v1, /device:TPU:1, one launch (start us, length us, event | category | flops | bytes accessed | tf_op | source)
XLA Modules:
  0.0 125.1 jit_solution(10513764889105250527)
XLA Ops:
  0.7 0.7 and_convert_fusion.pick_ref
  1.3 25.3 %reduce_pages.1 = bf16[32,3,128,128]{3,2,1,0:T(8,128)(2,1)} custom-call(s32[32]{0:T(128)} %lengths_ref.3, bf16[65536,128]{1,0:T(8,128)(2,1)} %bitcast.11, bf16[16,256]{1,0:T(8,128)(2,1)} %and_convert_fusion.pick_ref), custom_call_target="tpu_custom_call" | custom-call | tf_op jit(solution)/shard_map/reduce_pages/pallas_call | solution.py:137
  26.6 44.3 %all_to_all.10 = bf16[32,3,128,128]{3,2,1,0:T(8,128)(2,1)} all-to-all(bf16[32,3,128,128]{3,2,1,0:T(8,128)(2,1)} %reduce_pages.1), channel_id=1, replica_groups=mesh['head'=4,'seq'=32] {'seq'}, dimensions={0} | all-to-all | bytes 6291456 | tf_op jit(solution)/shard_map/all_to_all | solution.py:235
  70.9 0.0 copy-start.1
  70.9 6.8 %all-to-all-start.1 = ((bf16[4,8,3,128,128]{4,3,2,1,0:T(8,128)(2,1)}), bf16[4,8,3,128,128]{4,3,2,1,0:T(8,128)(2,1)S(1)}, u32[]{:S(2)}, u32[]{:S(2)}) async-start(bf16[4,8,3,128,128]{4,3,2,1,0:T(8,128)(2,1)} %bitcast.12), calls=%async_computation.1 | async-start | bytes 6291456 | tf_op jit(solution)/shard_map/all_to_all | solution.py:237
  77.7 0.0 copy-done.1
  77.7 0.0 collective-permute-start.2
  77.7 3.2 %collective-permute-start.1 = (bf16[16,128]{1,0:T(8,128)(2,1)S(1)}, bf16[16,128]{1,0:T(8,128)(2,1)S(1)}, u32[]{:S(2)}, u32[]{:S(2)}) collective-permute-start(bf16[16,128]{1,0:T(8,128)(2,1)S(1)} %bitcast.14), channel_id=1, source_target_pairs={{0,64},{32,96},{64,0},{96,32},{1,65},{33,97},{65,1},{97,33},{2,66}... | collective-permute-start | bytes 12296 | tf_op jit(solution)/shard_map/ppermute | solution.py:234
  81.0 3.1 %collective-permute-start = (bf16[16,128]{1,0:T(8,128)(2,1)S(1)}, bf16[16,128]{1,0:T(8,128)(2,1)S(1)}, u32[]{:S(2)}, u32[]{:S(2)}) collective-permute-start(bf16[16,128]{1,0:T(8,128)(2,1)S(1)} %bitcast.15), channel_id=1, source_target_pairs={{0,32},{32,64},{64,96},{96,0},{1,33},{33,65},{65,97},{97,1},{2,34}... | collective-permute-start | bytes 12296 | tf_op jit(solution)/shard_map/ppermute | solution.py:234
  84.1 31.7 %collective-permute-done.2 = bf16[16,128]{1,0:T(8,128)(2,1)S(1)} collective-permute-done((bf16[16,128]{1,0:T(8,128)(2,1)S(1)}, bf16[16,128]{1,0:T(8,128)(2,1)S(1)}, u32[]{:S(2)}, u32[]{:S(2)}) %collective-permute-start.2) | collective-permute-done | bytes 4128 | tf_op jit(solution)/shard_map/ppermute | solution.py:234
  115.8 0.0 collective-permute-done.1
  115.8 0.0 collective-permute-done
  115.8 0.6 pad_maximum_fusion.query_ref
  116.4 0.0 all-to-all-done.1.in_ref
  116.5 0.0 copy-start
  116.5 1.6 %copy-done = bf16[4,8,3,128,128]{4,3,2,1,0:T(8,128)(2,1)} copy-done((bf16[4,8,3,128,128]{4,3,2,1,0:T(8,128)(2,1)}, bf16[4,8,3,128,128]{4,3,2,1,0:T(8,128)(2,1)S(1)}, u32[]{:S(2)}) %copy-start) | copy-done | bytes 3145752
  118.1 7.1 %finish.1 = (bf16[4096,128]{1,0:T(8,128)(2,1)}, bf16[4096,128]{1,0:T(8,128)(2,1)}, f32[4096,128]{1,0:T(8,128)}, f32[64,512]{1,0:T(8,128)}) custom-call(s32[32]{0:T(128)} %lengths_ref.3, bf16[4,8,3,128,128]{4,3,2,1,0:T(8,128)(2,1)} %copy-done, bf16[4,16,128]{2,1,0:T(8,128)(2,1)} %pad_maximum_fusion.query_ref), custom_call_target="tpu_custom_call" | custom-call | tf_op jit(solution)/shard_map/finish/pallas_call | solution.py:204
  (2 shorter events, 0.0 us)
Async XLA Ops:
  70.9 6.8 %copy-start.1 = (bf16[1,16,128]{2,1,0:T(8,128)(2,1)S(1)}, bf16[1,16,128]{2,1,0:T(8,128)(2,1)}, u32[]{:S(2)}) copy-start(bf16[1,16,128]{2,1,0:T(8,128)(2,1)} %param.4) | copy-start | bytes 12292
  70.9 45.5 %all-to-all-start.1 = ((bf16[4,8,3,128,128]{4,3,2,1,0:T(8,128)(2,1)}), bf16[4,8,3,128,128]{4,3,2,1,0:T(8,128)(2,1)S(1)}, u32[]{:S(2)}, u32[]{:S(2)}) async-start(bf16[4,8,3,128,128]{4,3,2,1,0:T(8,128)(2,1)} %bitcast.12), calls=%async_computation.1 | async-start | bytes 6291456 | tf_op jit(solution)/shard_map/all_to_all | solution.py:237
  77.7 38.1 %collective-permute-start.2 = (bf16[16,128]{1,0:T(8,128)(2,1)S(1)}, bf16[16,128]{1,0:T(8,128)(2,1)S(1)}, u32[]{:S(2)}, u32[]{:S(2)}) collective-permute-start(bf16[16,128]{1,0:T(8,128)(2,1)S(1)} %bitcast.13), channel_id=1, source_target_pairs={{0,96},{32,0},{64,32},{96,64},{1,97},{33,1},{65,33},{97,65},{2,98}... | collective-permute-start | bytes 12296 | tf_op jit(solution)/shard_map/ppermute | solution.py:234
  77.7 38.1 %collective-permute-start.1 = (bf16[16,128]{1,0:T(8,128)(2,1)S(1)}, bf16[16,128]{1,0:T(8,128)(2,1)S(1)}, u32[]{:S(2)}, u32[]{:S(2)}) collective-permute-start(bf16[16,128]{1,0:T(8,128)(2,1)S(1)} %bitcast.14), channel_id=1, source_target_pairs={{0,64},{32,96},{64,0},{96,32},{1,65},{33,97},{65,1},{97,33},{2,66}... | collective-permute-start | bytes 12296 | tf_op jit(solution)/shard_map/ppermute | solution.py:234
  81.0 34.9 %collective-permute-start = (bf16[16,128]{1,0:T(8,128)(2,1)S(1)}, bf16[16,128]{1,0:T(8,128)(2,1)S(1)}, u32[]{:S(2)}, u32[]{:S(2)}) collective-permute-start(bf16[16,128]{1,0:T(8,128)(2,1)S(1)} %bitcast.15), channel_id=1, source_target_pairs={{0,32},{32,64},{64,96},{96,0},{1,33},{33,65},{65,97},{97,1},{2,34}... | collective-permute-start | bytes 12296 | tf_op jit(solution)/shard_map/ppermute | solution.py:234
  116.5 1.6 %copy-start = (bf16[4,8,3,128,128]{4,3,2,1,0:T(8,128)(2,1)}, bf16[4,8,3,128,128]{4,3,2,1,0:T(8,128)(2,1)S(1)}, u32[]{:S(2)}) copy-start(bf16[4,8,3,128,128]{4,3,2,1,0:T(8,128)(2,1)S(1)} %all-to-all-done.1.in_ref) | copy-start | bytes 9437188
